TPU v7x, 256 devices: a whole 4x4x8 slice. The times are simulated.
256 devices in a mesh: seq: 64 (over z, y, core), fsdp: 4 (over x).
Axes of the slice: x: 4, y: 4, z: 8, core: 2. Of those that a mesh axis runs over, the one named last changes fastest.
Arguments:
- inputs: bfloat16 [4, 8192, 3584], P('fsdp', 'seq'), may hold values from -36 to 36
- keys_queries: bfloat16 [4, 8192, 256], P('fsdp', 'seq'), may hold values from -0.29882812 to 0.29882812
- log_decay: float32 [4, 56, 8192], P('fsdp', None, 'seq'), may hold values from -1.5 to 0, as said below
- skip: float32 [56], replicated, may hold values from 0.5 to 1.5
- classifier: bfloat16 [3584, 128], P('fsdp'), may hold values from -0.09375 to 0.09375
Outputs:
- mixed: bfloat16 [4, 8192, 3584], P('fsdp', 'seq')
- logits: float32 [4, 128], P('fsdp')
Inputs may be any that keep to these rules, and one draw needn't show every extreme that they name: `log_decay`: log-decays are negative.
All inputs are finite; a program needn't handle non-finite values.
Results may differ from a plain program's by a relative error of at most 0.0051.
Values may be sent and summed in bfloat16 or wider, within the bound.
A program may use at most 256 MiB of HBM per device.

v0:
```python
import jax
import jax.numpy as jnp
from jax import lax
from jax.sharding import PartitionSpec as P

N = 128
GROUP = 128
epsilon = 1e-06


def linker(earlier, latter):
    return (earlier[0] + latter[0], jnp.exp(latter[0]) * earlier[1] + latter[1])


def local(inputs, keys_queries, log_decay, skip, classifier):
    copies, positions, channels = inputs.shape
    head_count = log_decay.shape[1]
    head_dim = channels // head_count
    blocks = positions // GROUP
    key_rows = keys_queries[:, :, :N].reshape(copies, blocks, GROUP, N)
    queries = keys_queries[:, :, N:].reshape(copies, blocks, GROUP, N)
    values = inputs.reshape(copies, blocks, GROUP, head_count, head_dim)
    cumulative = jnp.cumsum(log_decay.reshape(copies, head_count, blocks, GROUP), axis=-1)
    block_decay = cumulative[..., -1]
    weighted = (key_rows[:, None] * jnp.exp(block_decay[..., None] - cumulative)[..., None]).astype(
        jnp.bfloat16
    )
    block_state = jnp.einsum(
        "chkun,ckuhp->kchnp", weighted, values, preferred_element_type=jnp.float32
    )

    def advance(running, member):
        return (jnp.exp(member[0])[..., None, None] * running + member[1], running)

    device_state, starts = lax.scan(
        advance, jnp.zeros_like(block_state[0]), (jnp.moveaxis(block_decay, 2, 0), block_state)
    )
    device_decay = jnp.sum(block_decay, axis=-1)
    axis_count = lax.axis_size("seq")
    flattened = device_state.reshape(copies, head_count, 1, N * head_dim)
    decay_copies = jnp.broadcast_to(
        device_decay[:, :, None, None], (copies, head_count, 1, axis_count)
    )
    totals = lax.associative_scan(
        linker,
        (
            lax.all_to_all(decay_copies, "seq", split_axis=3, concat_axis=2, tiled=True),
            lax.all_to_all(flattened, "seq", split_axis=3, concat_axis=2, tiled=True),
        ),
        axis=2,
    )[1]
    shifted = jnp.concatenate([jnp.zeros_like(totals[:, :, :1]), totals[:, :, :-1]], axis=2)
    incoming = lax.all_to_all(shifted, "seq", split_axis=2, concat_axis=3, tiled=True)
    incoming = incoming.reshape(copies, head_count, N, head_dim)
    preceding = jnp.moveaxis(jnp.cumsum(block_decay, axis=-1) - block_decay, 2, 0)
    carried = (jnp.exp(preceding)[..., None, None] * incoming[None] + starts).astype(jnp.bfloat16)
    growth = jnp.exp(cumulative).transpose(0, 2, 3, 1)[..., None]
    carried_out = (
        jnp.einsum("ckqn,kchnp->ckqhp", queries, carried, preferred_element_type=jnp.float32)
        * growth
    )
    causal = jnp.arange(GROUP)[:, None] >= jnp.arange(GROUP)[None, :]
    scores = jnp.einsum("cktn,ckun->cktu", queries, key_rows, preferred_element_type=jnp.float32)
    decay_gap = jnp.where(causal, cumulative[..., :, None] - cumulative[..., None, :], -jnp.inf)
    mixing = (scores[:, None] * jnp.exp(decay_gap)).astype(jnp.bfloat16)
    diagonal = jnp.einsum("chktu,ckuhp->ckthp", mixing, values, preferred_element_type=jnp.float32)
    mixed_full = diagonal + carried_out + skip[:, None] * values.astype(jnp.float32)
    mixed = mixed_full.astype(jnp.bfloat16).reshape(copies, positions, channels)
    partial_sum = jnp.sum(mixed_full, axis=(1, 2)).reshape(copies, channels)
    pooled = lax.psum(partial_sum, "seq") / (positions * lax.axis_size("seq"))
    normed = (
        pooled / jnp.sqrt(jnp.mean(pooled * pooled, axis=-1, keepdims=True) + epsilon)
    ).astype(jnp.bfloat16)
    logits = jnp.dot(
        normed,
        lax.all_gather(classifier, "fsdp", axis=0, tiled=True),
        preferred_element_type=jnp.float32,
    )
    return (mixed, logits)


def solution(mesh):
    return jax.shard_map(
        local,
        mesh=mesh,
        in_specs=(
            P("fsdp", "seq", None),
            P("fsdp", "seq", None),
            P("fsdp", None, "seq"),
            P(),
            P("fsdp", None),
        ),
        out_specs=(P("fsdp", "seq", None), P("fsdp", None)),
        check_vma=False,
    )
```

profile of v0, /device:TPU:2, one launch (start us, length us, event | category | flops | bytes accessed | tf_op | source)
XLA Modules:
  0.0 497.6 jit_solution(18033312582586399048)
XLA Ops:
  0.6 1.1 reduce_window_sum.17
  1.7 0.2 multiply_reduce_fusion
  1.9 0.6 broadcast_in_dim.18
  2.5 12.1 %all-to-all-start.1 = ((f32[1,56,1,64]{1,2,0,3:T(1,128)}), f32[1,56,1,64]{1,2,0,3:T(1,128)S(1)}, u32[]{:S(2)}, u32[]{:S(2)}) async-start(f32[1,56,1,64]{1,2,0,3:T(1,128)} %broadcast_in_dim.18), calls=%async_computation.1 | async-start | bytes 65536 | tf_op jit(solution)/shard_map/all_to_all | solution.py:47
  14.7 0.1 subtract_exponential_fusion
  14.7 1.6 copy.45
  16.3 1.3 fusion.10
  17.6 4.5 copy.57
  22.1 0.5 broadcast.116
  22.6 38.4 %reduce.6 = f32[8192,56]{1,0:T(8,128)} reduce(f32[8192,1,1,56]{3,2,1,0:T(1,128)} %bitcast.76, f32[]{:T(128)} %broadcast.116), dimensions={1,2}, to_apply=%bitcast.65.reduce_sub_computation | reduce | bytes 3670020
  61.0 6.9 %reshape.245 = f32[64,1,7168]{2,1,0:T(1,128)} reshape(f32[8192,56]{1,0:T(8,128)} %reduce.6) | data formatting | bytes 3670016
  67.9 0.0 all-to-all-done.1
  67.9 10.5 %all-to-all-start = ((f32[64,1,7168]{2,1,0:T(1,128)}), f32[64,1,7168]{2,1,0:T(1,128)S(1)}, u32[]{:S(2)}, u32[]{:S(2)}) async-start(f32[64,1,7168]{2,1,0:T(1,128)} %reshape.245), calls=%async_computation | async-start | bytes 3670016 | tf_op jit(solution)/shard_map/all_to_all | solution.py:48
  78.8 45.2 %all-to-all-done = f32[64,1,7168]{2,1,0:T(1,128)S(1)} async-done(((f32[64,1,7168]{2,1,0:T(1,128)}), f32[64,1,7168]{2,1,0:T(1,128)S(1)}, u32[]{:S(2)}, u32[]{:S(2)}) %all-to-all-start) | async-done | bytes 1835040 | tf_op jit(solution)/shard_map/all_to_all | solution.py:48
  124.0 6.8 %reduce.7 = f32[64,7168]{1,0:T(8,128)} reduce(f32[64,1,7168]{2,1,0:T(1,128)S(1)} %all-to-all-done, f32[]{:T(128)} %broadcast.116), dimensions={1}, to_apply=%all_to_all.10.reduce_sub_computation | reduce | bytes 3670020 | tf_op jit(solution)/shard_map/all_to_all | solution.py:48
  130.7 11.1 %reshape.246 = f32[8192,1,1,56]{3,2,1,0:T(1,128)} reshape(f32[64,7168]{1,0:T(8,128)} %reduce.7) | data formatting | bytes 3670016
  141.8 4.1 fusion.34
  145.9 1.5 slice.192
  147.4 0.6 slice.195
  148.0 2.2 copy.60
  150.2 1.5 copy.61
  151.7 1.5 multiply_add_fusion
  153.2 0.2 slice_add_fusion
  153.4 0.1 slice_add_fusion.1
  153.5 0.1 slice_add_fusion.2
  153.6 0.1 slice_add_fusion.3
  153.7 0.1 fusion.37
  153.8 0.1 fusion.36
  154.0 0.1 fusion.14
  154.2 0.1 pad.45
  154.3 0.1 fusion.13
  154.5 0.1 pad.44
  154.6 0.2 fusion.12
  154.9 0.2 pad.46
  155.0 0.4 pad.47
  155.4 0.0 copy-start.2
  155.5 0.9 copy-done.2
  156.4 1.0 add.138
  157.4 16.4 %pad.85 = f32[1,56,64,128]{3,1,0,2:T(8,128)} pad(f32[1,56,32,128]{3,1,0,2:T(8,128)} %add.138, f32[]{:T(128)} %constant.16.clone.1), padding=0_0_0x0_0_0x1_0_1x0_0_0 | pad | bytes 2752516
  173.8 1.5 copy.62
  175.3 0.1 copy.59
  175.4 1.8 fusion.11
  177.2 0.1 pad_maximum_fusion
  177.2 11.0 %pad.61 = f32[1,56,63,128]{3,1,0,2:T(8,128)} pad(f32[1,56,32,128]{3,1,0,2:T(8,128)S(1)} %pad_maximum_fusion, f32[]{:T(128)} %constant.16.clone.1), padding=0_0_0x0_0_0x0_0_1x0_0_0 | pad | bytes 2723844 | tf_op jit(solution)/shard_map/slice | solution.py:52
  188.3 1.7 slice_add_fusion.5
  190.0 1.3 concatenate.23
  191.3 5.3 %all-to-all-start.2 = ((f32[1,56,64,128]{3,1,0,2:T(8,128)}), f32[1,56,64,128]{3,1,0,2:T(8,128)S(1)}, u32[]{:S(2)}, u32[]{:S(2)}) async-start(f32[1,56,64,128]{3,1,0,2:T(8,128)} %concatenate.23), calls=%async_computation.2 | async-start | bytes 3670016 | tf_op jit(solution)/shard_map/all_to_all | solution.py:53
  196.6 2.6 copy.54
  199.3 0.1 fusion.16
  199.4 0.0 copy-start.10
  199.4 2.6 fusion
  202.0 15.5 %all_gather.3 = bf16[3584,128]{1,0:T(8,128)(2,1)} all-gather(bf16[896,128]{1,0:T(8,128)(2,1)S(1)} %copy-done.10), channel_id=1, replica_groups=mesh['seq'=64,'fsdp'=4] {'fsdp'}, dimensions={0}, use_global_device_ids=true | all-gather | bytes 1146880 | tf_op jit(solution)/shard_map/all_gather | solution.py:76
  217.5 24.9 %all-to-all-done.2 = f32[1,56,64,128]{3,1,0,2:T(8,128)S(1)} async-done(((f32[1,56,64,128]{3,1,0,2:T(8,128)}), f32[1,56,64,128]{3,1,0,2:T(8,128)S(1)}, u32[]{:S(2)}, u32[]{:S(2)}) %all-to-all-start.2) | async-done | bytes 1835040 | tf_op jit(solution)/shard_map/all_to_all | solution.py:53
  242.4 0.2 multiply_convert_fusion.4
  242.6 0.2 copy.52
  242.8 0.0 copy-start.11
  242.8 1.7 convert_element_type.57
  244.6 0.0 copy-done.3
  244.6 3.3 fusion.35
  247.9 0.1 reshape.236
  248.0 246.3 %psum.7 = f32[1,3584]{1,0:T(1,128)S(1)} all-reduce(f32[1,3584]{1,0:T(1,128)S(1)} %reshape.236), channel_id=1, replica_groups=mesh['seq'=64,'fsdp'=4] {'seq'}, use_global_device_ids=true, to_apply=%region_2.3 | all-reduce | flops 3584 | bytes 28672 | tf_op jit(solution)/shard_map/psum | solution.py:70
  494.3 0.6 multiply_reduce_fusion.1
  495.6 1.3 copy.55
  496.9 0.7 fusion.25
  (63 shorter events, 0.7 us)
Async XLA Ops:
  0.6 15.7 %copy-start.8 = (bf16[1,128,256]{2,1,0:T(8,128)(2,1)S(1)}, bf16[1,128,256]{2,1,0:T(8,128)(2,1)}, u32[]{:S(2)}) copy-start(bf16[1,128,256]{2,1,0:T(8,128)(2,1)} %param.6) | copy-start | bytes 196612
  2.5 65.4 %all-to-all-start.1 = ((f32[1,56,1,64]{1,2,0,3:T(1,128)}), f32[1,56,1,64]{1,2,0,3:T(1,128)S(1)}, u32[]{:S(2)}, u32[]{:S(2)}) async-start(f32[1,56,1,64]{1,2,0,3:T(1,128)} %broadcast_in_dim.18), calls=%async_computation.1 | async-start | bytes 65536 | tf_op jit(solution)/shard_map/all_to_all | solution.py:47
  16.3 5.8 %copy-start.5 = (bf16[1,128,3584]{1,2,0:T(8,128)(2,1)}, bf16[1,128,3584]{1,2,0:T(8,128)(2,1)S(1)}, u32[]{:S(2)}) copy-start(bf16[1,128,3584]{1,2,0:T(8,128)(2,1)S(1)} %copy.45) | copy-start | bytes 2752516
  67.9 56.0 %all-to-all-start = ((f32[64,1,7168]{2,1,0:T(1,128)}), f32[64,1,7168]{2,1,0:T(1,128)S(1)}, u32[]{:S(2)}, u32[]{:S(2)}) async-start(f32[64,1,7168]{2,1,0:T(1,128)} %reshape.245), calls=%async_computation | async-start | bytes 3670016 | tf_op jit(solution)/shard_map/all_to_all | solution.py:48
  141.8 4.1 copy-start
  155.4 0.9 copy-start.2
  157.4 16.4 %copy-start.1 = (f32[1,56,31,128]{1,3,2,0:T(8,128)S(1)}, f32[1,56,31,128]{1,3,2,0:T(8,128)}, u32[]{:S(2)}) copy-start(f32[1,56,31,128]{1,3,2,0:T(8,128)} %slice.192) | copy-start | bytes 2666500
  173.8 1.5 copy-start.9
  177.2 11.1 %copy-start.4 = (f32[1,56,64,128]{3,1,0,2:T(8,128)S(1)}, f32[1,56,64,128]{3,1,0,2:T(8,128)}, u32[]{:S(2)}) copy-start(f32[1,56,64,128]{3,1,0,2:T(8,128)} %pad.85) | copy-start | bytes 5505028
  191.3 51.1 %all-to-all-start.2 = ((f32[1,56,64,128]{3,1,0,2:T(8,128)}), f32[1,56,64,128]{3,1,0,2:T(8,128)S(1)}, u32[]{:S(2)}, u32[]{:S(2)}) async-start(f32[1,56,64,128]{3,1,0,2:T(8,128)} %concatenate.23), calls=%async_computation.2 | async-start | bytes 3670016 | tf_op jit(solution)/shard_map/all_to_all | solution.py:53
  196.6 2.8 copy-start.6
  199.4 2.6 copy-start.10
  242.8 1.8 copy-start.3
  242.8 1.8 copy-start.11
  247.9 249.0 %copy-start.7 = (bf16[3584,128]{1,0:T(8,128)(2,1)S(1)}, bf16[3584,128]{1,0:T(8,128)(2,1)}, u32[]{:S(2)}) copy-start(bf16[3584,128]{1,0:T(8,128)(2,1)} %all_gather.3) | copy-start | bytes 2752516
where the time goes:
time: 500 us; the launch traced here: 498 us
  blocking collectives  262 us (52%)
  local copies, waits for them, and re-layouts  73.5 us (15%)
  waiting for transfers between devices  70.1 us (14%)
  other arithmetic  54.6 us (11%)
  starting transfers between devices  27.9 us (6%)
  matrix products  7.99 us (2%)
    psum x1, blocking collectives, local(): pooled = lax.psum(partial_sum, 'seq') / (positions * lax.axis_size('seq'))  246 us
    all_to_all x1, waiting for transfers between devices, local(): lax.all_to_all(flattened, 'seq', split_axis=3, concat_axis=2, tiled=True)  45.2 us
    unnamed x34, local copies, waits for them, and re-layouts  44 us
    unnamed x1, other arithmetic  38.4 us
    all_to_all x1, waiting for transfers between devices, local(): lax.all_to_all(shifted, 'seq', split_axis=2, concat_axis=3, tiled=True)  24.9 us
    all_gather x1, blocking collectives, local(): lax.all_gather(classifier, 'fsdp', axis=0, tiled=True)  15.5 us
    all_to_all x1, starting transfers between devices, local(): lax.all_to_all(decay_copies, 'seq', split_axis=3, concat_axis=2, tiled=True)  12.1 us
    slice x1, local copies, waits for them, and re-layouts, local(): totals[:, :, :-1]  11 us
  transfers between devices with their start and end apart: 3, of which 2 were waited for; matrix products, arithmetic and copies ran while one was open for 12% of the time, Pallas kernels for 0%

commit v1 on v0

--- a/solution.py
+++ b/solution.py
@@ -6,6 +6,27 @@
 N = 128
 GROUP = 128
 epsilon = 1e-06
+
+
+def ring_gather(value, axis, dim):
+    devices, mine, rows = (lax.axis_size(axis), lax.axis_index(axis), value.shape[dim])
+    upward = [(i, (i + 1) % devices) for i in range(devices)]
+    left = [(i, (i - 1) % devices) for i in range(devices)]
+    whole = jnp.zeros((*value.shape[:dim], devices * rows, *value.shape[dim + 1 :]), value.dtype)
+    whole = lax.dynamic_update_slice_in_dim(whole, value, mine * rows, axis=dim)
+    from_left = from_right = value
+    half = devices // 2
+    for step in range(1, half + 1):
+        from_left = lax.ppermute(from_left, axis, upward)
+        whole = lax.dynamic_update_slice_in_dim(
+            whole, from_left, (mine - step) % devices * rows, axis=dim
+        )
+        if step < devices - half:
+            from_right = lax.ppermute(from_right, axis, left)
+            whole = lax.dynamic_update_slice_in_dim(
+                whole, from_right, (mine + step) % devices * rows, axis=dim
+            )
+    return whole
 
 
 def linker(earlier, latter):
@@ -71,11 +92,7 @@
     normed = (
         pooled / jnp.sqrt(jnp.mean(pooled * pooled, axis=-1, keepdims=True) + epsilon)
     ).astype(jnp.bfloat16)
-    logits = jnp.dot(
-        normed,
-        lax.all_gather(classifier, "fsdp", axis=0, tiled=True),
-        preferred_element_type=jnp.float32,
-    )
+    logits = jnp.dot(normed, ring_gather(classifier, "fsdp", 0), preferred_element_type=jnp.float32)
     return (mixed, logits)
 
 

time: 500 us -> 501 us (level)
  blocking collectives: 262 us -> 246 us
  waiting for transfers between devices: 70.1 us -> 77.2 us
    all_gather x1 -> x0, blocking collectives: 15.5 us -> none  [local(): lax.all_gather(classifier, 'fsdp', axis=0, tiled=True)]
    unnamed x34 -> x32, local copies, waits for them, and re-layouts: 44 us -> 43.9 us
  transfers between devices with their start and end apart: 3 -> 6, of which waited for: 2 -> 3; matrix products, arithmetic and copies ran while one was open for 12% -> 13% of each run, Pallas kernels for 0% -> 0%
where the time goes in v1:
time: 501 us; the launch traced here: 499 us
  blocking collectives  246 us (49%)
  local copies, waits for them, and re-layouts  78.2 us (16%)
  waiting for transfers between devices  77.2 us (15%)
  other arithmetic  54.6 us (11%)
  starting transfers between devices  31.7 us (6%)
  matrix products  9.16 us (2%)
    psum x1, blocking collectives, local(): pooled = lax.psum(partial_sum, 'seq') / (positions * lax.axis_size('seq'))  246 us
    all_to_all x1, waiting for transfers between devices, local(): lax.all_to_all(flattened, 'seq', split_axis=3, concat_axis=2, tiled=True)  45.2 us
    unnamed x32, local copies, waits for them, and re-layouts  43.9 us
    unnamed x1, other arithmetic  38.4 us
    all_to_all x1, waiting for transfers between devices, local(): lax.all_to_all(shifted, 'seq', split_axis=2, concat_axis=3, tiled=True)  28.9 us
    all_to_all x1, starting transfers between devices, local(): lax.all_to_all(decay_copies, 'seq', split_axis=3, concat_axis=2, tiled=True)  12.1 us
    slice x1, local copies, waits for them, and re-layouts, local(): totals[:, :, :-1]  11 us
    all_to_all x1, starting transfers between devices, local(): lax.all_to_all(flattened, 'seq', split_axis=3, concat_axis=2, tiled=True)  10.5 us
  transfers between devices with their start and end apart: 6, of which 3 were waited for; matrix products, arithmetic and copies ran while one was open for 13% of the time, Pallas kernels for 0%

profile of v1, /device:TPU:2, one launch (start us, length us, event | category | flops | bytes accessed | tf_op | source)
XLA Modules:
  0.0 498.8 jit_solution(2659656904368252162)
XLA Ops:
  0.6 1.1 reduce_window_sum.17
  1.7 0.2 multiply_reduce_fusion
  1.9 0.6 broadcast_in_dim.20
  2.5 12.1 %all-to-all-start.1 = ((f32[1,56,1,64]{1,2,0,3:T(1,128)}), f32[1,56,1,64]{1,2,0,3:T(1,128)S(1)}, u32[]{:S(2)}, u32[]{:S(2)}) async-start(f32[1,56,1,64]{1,2,0,3:T(1,128)} %broadcast_in_dim.20), calls=%async_computation.1 | async-start | bytes 65536 | tf_op jit(solution)/shard_map/all_to_all | solution.py:68
  14.7 0.1 subtract_exponential_fusion
  14.7 1.6 copy.45
  16.3 1.3 fusion.10
  17.6 4.5 copy.57
  22.1 0.5 broadcast.119
  22.6 38.4 %reduce.6 = f32[8192,56]{1,0:T(8,128)} reduce(f32[8192,1,1,56]{3,2,1,0:T(1,128)} %bitcast.76, f32[]{:T(128)} %broadcast.119), dimensions={1,2}, to_apply=%bitcast.65.reduce_sub_computation | reduce | bytes 3670020
  61.0 6.9 %reshape.245 = f32[64,1,7168]{2,1,0:T(1,128)} reshape(f32[8192,56]{1,0:T(8,128)} %reduce.6) | data formatting | bytes 3670016
  67.9 10.5 %all-to-all-start = ((f32[64,1,7168]{2,1,0:T(1,128)}), f32[64,1,7168]{2,1,0:T(1,128)S(1)}, u32[]{:S(2)}, u32[]{:S(2)}) async-start(f32[64,1,7168]{2,1,0:T(1,128)} %reshape.245), calls=%async_computation | async-start | bytes 3670016 | tf_op jit(solution)/shard_map/all_to_all | solution.py:69
  78.8 45.2 %all-to-all-done = f32[64,1,7168]{2,1,0:T(1,128)S(1)} async-done(((f32[64,1,7168]{2,1,0:T(1,128)}), f32[64,1,7168]{2,1,0:T(1,128)S(1)}, u32[]{:S(2)}, u32[]{:S(2)}) %all-to-all-start) | async-done | bytes 1835040 | tf_op jit(solution)/shard_map/all_to_all | solution.py:69
  124.0 6.8 %reduce.7 = f32[64,7168]{1,0:T(8,128)} reduce(f32[64,1,7168]{2,1,0:T(1,128)S(1)} %all-to-all-done, f32[]{:T(128)} %broadcast.119), dimensions={1}, to_apply=%all_to_all.10.reduce_sub_computation | reduce | bytes 3670020 | tf_op jit(solution)/shard_map/all_to_all | solution.py:69
  130.7 11.1 %reshape.246 = f32[8192,1,1,56]{3,2,1,0:T(1,128)} reshape(f32[64,7168]{1,0:T(8,128)} %reduce.7) | data formatting | bytes 3670016
  141.8 4.1 fusion.34
  145.9 1.5 slice.192
  147.4 0.6 slice.195
  148.0 2.2 copy.60
  150.2 1.5 copy.61
  151.7 1.5 multiply_add_fusion
  153.2 0.2 slice_add_fusion
  153.4 0.1 slice_add_fusion.1
  153.5 0.1 slice_add_fusion.2
  153.6 0.1 slice_add_fusion.3
  153.8 0.1 fusion.36
  154.0 0.1 fusion.14
  154.2 0.1 pad.45
  154.3 0.1 fusion.13
  154.5 0.1 pad.44
  154.6 0.2 fusion.12
  154.8 0.2 pad.46
  155.0 0.4 pad.47
  155.4 0.9 copy-done.2
  156.3 1.0 add.165
  157.4 16.4 %pad.85 = f32[1,56,64,128]{3,1,0,2:T(8,128)} pad(f32[1,56,32,128]{3,1,0,2:T(8,128)} %add.165, f32[]{:T(128)} %constant.57.clone.1), padding=0_0_0x0_0_0x1_0_1x0_0_0 | pad | bytes 2752516
  173.8 1.5 copy.62
  175.4 1.8 fusion.11
  177.2 11.0 %pad.61 = f32[1,56,63,128]{3,1,0,2:T(8,128)} pad(f32[1,56,32,128]{3,1,0,2:T(8,128)S(1)} %pad_maximum_fusion, f32[]{:T(128)} %constant.57.clone.1), padding=0_0_0x0_0_0x0_0_1x0_0_0 | pad | bytes 2723844 | tf_op jit(solution)/shard_map/slice | solution.py:73
  188.2 1.7 slice_add_fusion.5
  189.9 1.4 concatenate.23
  191.3 5.5 %all-to-all-start.2 = ((f32[1,56,64,128]{3,1,0,2:T(8,128)}), f32[1,56,64,128]{3,1,0,2:T(8,128)S(1)}, u32[]{:S(2)}, u32[]{:S(2)}) async-start(f32[1,56,64,128]{3,1,0,2:T(8,128)} %concatenate.23), calls=%async_computation.2 | async-start | bytes 3670016 | tf_op jit(solution)/shard_map/all_to_all | solution.py:74
  196.8 1.6 collective-permute-start
  198.3 0.5 collective-permute-start.1
  198.9 0.1 fusion.16
  199.0 2.6 fusion
  201.6 2.5 copy.54
  204.1 1.1 broadcast_in_dim.23
  205.2 0.7 constant_dynamic-update-slice_fusion.3
  205.9 1.5 collective-permute-start.2
  207.4 0.7 constant_dynamic-update-slice_fusion.2
  208.1 1.7 constant_dynamic-update-slice_fusion.1
  209.8 3.1 collective-permute-done.2
  212.9 0.7 constant_dynamic-update-slice_fusion
  213.6 28.9 %all-to-all-done.2 = f32[1,56,64,128]{3,1,0,2:T(8,128)S(1)} async-done(((f32[1,56,64,128]{3,1,0,2:T(8,128)}), f32[1,56,64,128]{3,1,0,2:T(8,128)S(1)}, u32[]{:S(2)}, u32[]{:S(2)}) %all-to-all-start.2) | async-done | bytes 1835040 | tf_op jit(solution)/shard_map/all_to_all | solution.py:74
  242.5 0.2 multiply_convert_fusion.4
  242.7 0.2 copy.52
  243.0 1.8 convert_element_type.57
  244.7 3.3 fusion.35
  248.0 0.1 reshape.236
  248.1 246.2 %psum.7 = f32[1,3584]{1,0:T(1,128)S(1)} all-reduce(f32[1,3584]{1,0:T(1,128)S(1)} %reshape.236), channel_id=1, replica_groups=mesh['seq'=64,'fsdp'=4] {'seq'}, use_global_device_ids=true, to_apply=%region_2.3 | all-reduce | flops 3584 | bytes 28672 | tf_op jit(solution)/shard_map/psum | solution.py:91
  494.2 0.6 multiply_reduce_fusion.1
  495.6 1.3 copy.55
  496.8 1.9 fusion.25
  (71 shorter events, 0.9 us)
Async XLA Ops:
  0.6 15.7 %copy-start.7 = (bf16[1,128,256]{2,1,0:T(8,128)(2,1)S(1)}, bf16[1,128,256]{2,1,0:T(8,128)(2,1)}, u32[]{:S(2)}) copy-start(bf16[1,128,256]{2,1,0:T(8,128)(2,1)} %param.6) | copy-start | bytes 196612
  2.5 65.4 %all-to-all-start.1 = ((f32[1,56,1,64]{1,2,0,3:T(1,128)}), f32[1,56,1,64]{1,2,0,3:T(1,128)S(1)}, u32[]{:S(2)}, u32[]{:S(2)}) async-start(f32[1,56,1,64]{1,2,0,3:T(1,128)} %broadcast_in_dim.20), calls=%async_computation.1 | async-start | bytes 65536 | tf_op jit(solution)/shard_map/all_to_all | solution.py:68
  16.3 5.8 %copy-start.5 = (bf16[1,128,3584]{1,2,0:T(8,128)(2,1)}, bf16[1,128,3584]{1,2,0:T(8,128)(2,1)S(1)}, u32[]{:S(2)}) copy-start(bf16[1,128,3584]{1,2,0:T(8,128)(2,1)S(1)} %copy.45) | copy-start | bytes 2752516
  67.9 56.0 %all-to-all-start = ((f32[64,1,7168]{2,1,0:T(1,128)}), f32[64,1,7168]{2,1,0:T(1,128)S(1)}, u32[]{:S(2)}, u32[]{:S(2)}) async-start(f32[64,1,7168]{2,1,0:T(1,128)} %reshape.245), calls=%async_computation | async-start | bytes 3670016 | tf_op jit(solution)/shard_map/all_to_all | solution.py:69
  141.8 4.1 copy-start
  155.4 0.9 copy-start.2
  157.4 16.4 %copy-start.1 = (f32[1,56,31,128]{1,3,2,0:T(8,128)S(1)}, f32[1,56,31,128]{1,3,2,0:T(8,128)}, u32[]{:S(2)}) copy-start(f32[1,56,31,128]{1,3,2,0:T(8,128)} %slice.192) | copy-start | bytes 2666500
  173.8 1.5 copy-start.8
  177.1 11.1 %copy-start.4 = (f32[1,56,64,128]{3,1,0,2:T(8,128)S(1)}, f32[1,56,64,128]{3,1,0,2:T(8,128)}, u32[]{:S(2)}) copy-start(f32[1,56,64,128]{3,1,0,2:T(8,128)} %pad.85) | copy-start | bytes 5505028
  191.3 5.5 %copy-start.9 = (bf16[896,128]{1,0:T(8,128)(2,1)S(1)}, bf16[896,128]{1,0:T(8,128)(2,1)}, u32[]{:S(2)}) copy-start(bf16[896,128]{1,0:T(8,128)(2,1)} %param.9) | copy-start | bytes 688132
  191.3 7.8 %copy-start.6 = (bf16[1,128,3584]{1,2,0:T(8,128)(2,1)S(1)}, bf16[1,128,3584]{1,2,0:T(8,128)(2,1)}, u32[]{:S(2)}) copy-start(bf16[1,128,3584]{1,2,0:T(8,128)(2,1)} %copy-done.5) | copy-start | bytes 2752516
  191.3 51.2 %all-to-all-start.2 = ((f32[1,56,64,128]{3,1,0,2:T(8,128)}), f32[1,56,64,128]{3,1,0,2:T(8,128)S(1)}, u32[]{:S(2)}, u32[]{:S(2)}) async-start(f32[1,56,64,128]{3,1,0,2:T(8,128)} %concatenate.23), calls=%async_computation.2 | async-start | bytes 3670016 | tf_op jit(solution)/shard_map/all_to_all | solution.py:74
  196.8 9.1 %collective-permute-start = (bf16[896,128]{1,0:T(8,128)(2,1)S(1)}, bf16[896,128]{1,0:T(8,128)(2,1)S(1)}, u32[]{:S(2)}, u32[]{:S(2)}) collective-permute-start(bf16[896,128]{1,0:T(8,128)(2,1)S(1)} %copy-done.9), channel_id=1, source_target_pairs={{0,1},{1,2},{2,3},{3,0},{4,5},{5,6},{6,7},{7,4},{8,9},{9,10},{10,1... | collective-permute-start | bytes 688136 | tf_op jit(solution)/shard_map/ppermute | solution.py:20
  198.3 9.8 %collective-permute-start.1 = (bf16[896,128]{1,0:T(8,128)(2,1)S(1)}, bf16[896,128]{1,0:T(8,128)(2,1)}, u32[]{:S(2)}, u32[]{:S(2)}) collective-permute-start(bf16[896,128]{1,0:T(8,128)(2,1)S(1)} %copy-done.9), channel_id=1, source_target_pairs={{0,3},{1,0},{2,1},{3,2},{4,7},{5,4},{6,5},{7,6},{8,11},{9,8},{10,9... | collective-permute-start | bytes 688136 | tf_op jit(solution)/shard_map/ppermute | solution.py:25
  205.9 7.0 %collective-permute-start.2 = (bf16[896,128]{1,0:T(8,128)(2,1)S(1)}, bf16[896,128]{1,0:T(8,128)(2,1)S(1)}, u32[]{:S(2)}, u32[]{:S(2)}) collective-permute-start(bf16[896,128]{1,0:T(8,128)(2,1)S(1)} %collective-permute-done), channel_id=1, source_target_pairs={{0,1},{1,2},{2,3},{3,0},{4,5},{5,6},{6,7},{7,4},{8,9},{9,10},{10,1... | collective-permute-start | bytes 688136 | tf_op jit(solution)/shard_map/ppermute | solution.py:20
  242.9 1.8 copy-start.3
  242.9 1.8 copy-start.10
